TPU v7x, 256 devices: a whole 4x4x8 slice. The times are simulated.
256 devices in a mesh: wide: 64 (over z_hi, x, y, core), narrow: 4 (over z_lo).
Axes of the slice: x: 4, y: 4, z: 8 (z_hi: 2, z_lo: 4; z = z_hi * 4 + z_lo), core: 2. Of those that a mesh axis runs over, the one named last changes fastest.
Arguments:
- factor_rows: float32 [1, 4, 4, 64, 16, 1024], P(None, 'narrow', None, 'wide'), may hold values from -0.09375 to 0.09375
- load_vectors: float32 [1, 4, 1024, 128], P(None, 'narrow', 'wide'), may hold values from -6 to 6
- child_updates: float32 [4, 1, 4, 1024, 128], P('narrow', None, None, 'wide'), may hold values from -4 to 4
- block_inverses: float32 [4, 1024, 1024], P(None, 'wide'), may hold values from -1 to 2, as said below
Outputs:
- forward_solution: float32 [1, 4, 1024, 128], P(None, 'narrow', 'wide')
Inputs may be any that keep to these rules, and one draw needn't show every extreme that they name: Each block of block_inverses has a diagonal between 0.4 and 1.6.
All inputs are finite; a program needn't handle non-finite values.
Results may differ from a plain program's by a relative error of at most 0.0001.
Values sent between devices are 32-bit elements; how exact they have to be, the bound alone decides.
A program may use at most 64 MiB of HBM per device.

v0:
```python
import jax
import jax.numpy as jnp
from jax import lax
from jax.sharding import PartitionSpec as P


def from_root(shard, axis, root):
    mine = lax.axis_index(axis) == root
    return lax.psum(jnp.where(mine, shard, jnp.zeros_like(shard)), axis)


def body(factor_rows, load_vectors, child_updates, block_inverses):
    blocks_dev = factor_rows.shape[0]
    narrow_count = lax.axis_size("narrow")
    block_count = blocks_dev * narrow_count
    sub_rows = factor_rows.shape[4]
    block_width = factor_rows.shape[5]
    case_count = load_vectors.shape[3]
    my_lane = lax.axis_index("narrow")
    panel = factor_rows.reshape(blocks_dev, block_count, sub_rows, block_width)
    kid_sums = lax.psum_scatter(child_updates, "narrow", scatter_dimension=2, tiled=True)
    given_part = load_vectors.reshape(blocks_dev, sub_rows, case_count) - kid_sums.reshape(
        blocks_dev, sub_rows, case_count
    )
    solved = jnp.zeros((block_count, sub_rows, case_count), jnp.float32)
    held_sums = jnp.zeros((blocks_dev, block_width, case_count), jnp.float32)

    def advance(block_index, state_pair):
        solved, held_sums = state_pair
        own_block = block_index // narrow_count
        owner = block_index % narrow_count
        rows_here = lax.dynamic_index_in_dim(panel, own_block, 0, keepdims=False)
        reduced = lax.psum_scatter(
            jnp.einsum("cqr,cqk->rk", rows_here, solved, precision=lax.Precision.HIGHEST),
            "wide",
            scatter_dimension=0,
            tiled=True,
        )
        residual_part = lax.dynamic_index_in_dim(given_part, own_block, 0, keepdims=False) - reduced
        inverse_rows = lax.dynamic_index_in_dim(block_inverses, block_index, 0, keepdims=False)
        residual_full = lax.all_gather(residual_part, "wide", axis=0, tiled=True)
        applied = jnp.dot(
            inverse_rows,
            residual_full,
            precision=lax.Precision.HIGHEST,
            preferred_element_type=jnp.float32,
        )
        newest = from_root(applied, "narrow", owner)
        solved = lax.dynamic_update_index_in_dim(solved, newest, block_index, 0)
        return (solved, held_sums)

    solved, held_sums = lax.fori_loop(0, block_count, advance, (solved, held_sums))
    arranged = solved.reshape(blocks_dev, narrow_count, sub_rows, case_count)
    return lax.dynamic_slice_in_dim(arranged, my_lane, 1, 1)


def solution(mesh):
    placed = (
        P(None, "narrow", None, "wide", None, None),
        P(None, "narrow", "wide", None),
        P("narrow", None, None, "wide", None),
        P(None, "wide", None),
    )
    return jax.shard_map(
        body, mesh=mesh, in_specs=placed, out_specs=P(None, "narrow", "wide", None), check_vma=False
    )
```

profile of v0, /device:TPU:96, one launch (start us, length us, event | category | flops | bytes accessed | tf_op | source)
XLA Modules:
  0.0 2168.7 jit_solution(16757187029783483254)
XLA Ops:
  6.5 0.0 reduce-scatter.3.cloned.1.call-start
  6.5 0.7 reduce-scatter.3.cloned.1.call-update
  7.3 0.0 copy-start
  7.3 25.7 %reduce-scatter.3.cloned.1.call-done = f32[1,1,1,16,128]{4,3,2,1,0:T(8,128)} async-done(((f32[1,1,4,16,128]{4,3,2,1,0:T(8,128)}), f32[1,1,1,16,128]{4,3,2,1,0:T(8,128)}) %reduce-scatter.3.cloned.1.call-update) | async-done | bytes 8208 | tf_op jit(solution)/shard_map/reduce_scatter | solution.py:21
  33.0 0.0 copy-done
  33.0 0.7 bitcast_subtract_fusion.1
  33.7 2127.9 %while.15 = (s32[]{:T(128)}, f32[4,16,128]{2,1,0:T(8,128)S(1)}, f32[4,16,1024]{2,1,0:T(8,128)}, f32[1,16,128]{2,1,0:T(8,128)S(1)}, f32[1,4,16,1024]{3,2,1,0:T(8,...) while((s32[]{:T(128)}, f32[4,16,128]{2,1,0:T(8,128)S(1)}, f32[4,16,1024]{2,1,0:T(8,128)}, ...), condition=%wide.region_4.5_spmd, body=%wide.region_1.4_spmd.sunk | while | flops 125835264 | bytes 3604725 | solution.py:52
  33.7 0.0 reduce-scatter.5.cloned.1.call-start
  33.7 2.7 convolution_bitcast_fusion.2
  36.5 0.0 reduce-scatter.5.cloned.1.call-update
  36.5 412.7 %reduce-scatter.5.cloned.1.call-done = f32[16,128]{1,0:T(8,128)} async-done(((f32[1024,128]{1,0:T(8,128)}), f32[16,128]{1,0:T(8,128)}) %reduce-scatter.5.cloned.1.call-update) | async-done | bytes 8208 | tf_op jit(solution)/shard_map/while/body/eval_jaxpr/reduce_scatter | solution.py:33
  449.2 0.7 bitcast_subtract_fusion.3
  449.9 108.9 %all_gather.11 = f32[1024,128]{1,0:T(8,128)S(1)} all-gather(f32[16,128]{1,0:T(8,128)S(1)} %bitcast_subtract_fusion.3), channel_id=1, replica_groups=mesh['wide'=64,'narrow'=4] {'wide'}, dimensions={0}, use_global_device_ids=true | all-gather | bytes 532480 | tf_op jit(solution)/shard_map/while/body/eval_jaxpr/all_gather | solution.py:41
  558.8 1.2 fusion.16
  560.0 8.7 psum.15
  568.8 0.0 reduce-scatter.5.cloned.1.call-start
  568.8 2.7 convolution_bitcast_fusion.2
  571.5 0.0 reduce-scatter.5.cloned.1.call-update
  571.6 408.5 %reduce-scatter.5.cloned.1.call-done = f32[16,128]{1,0:T(8,128)} async-done(((f32[1024,128]{1,0:T(8,128)}), f32[16,128]{1,0:T(8,128)}) %reduce-scatter.5.cloned.1.call-update) | async-done | bytes 8208 | tf_op jit(solution)/shard_map/while/body/eval_jaxpr/reduce_scatter | solution.py:33
  980.1 0.7 bitcast_subtract_fusion.3
  980.8 108.8 %all_gather.11 = f32[1024,128]{1,0:T(8,128)S(1)} all-gather(f32[16,128]{1,0:T(8,128)S(1)} %bitcast_subtract_fusion.3), channel_id=1, replica_groups=mesh['wide'=64,'narrow'=4] {'wide'}, dimensions={0}, use_global_device_ids=true | all-gather | bytes 532480 | tf_op jit(solution)/shard_map/while/body/eval_jaxpr/all_gather | solution.py:41
  1089.6 1.2 fusion.16
  1090.8 9.7 psum.15
  1100.5 0.0 reduce-scatter.5.cloned.1.call-start
  1100.6 2.7 convolution_bitcast_fusion.2
  1103.3 0.0 reduce-scatter.5.cloned.1.call-update
  1103.3 407.3 %reduce-scatter.5.cloned.1.call-done = f32[16,128]{1,0:T(8,128)} async-done(((f32[1024,128]{1,0:T(8,128)}), f32[16,128]{1,0:T(8,128)}) %reduce-scatter.5.cloned.1.call-update) | async-done | bytes 8208 | tf_op jit(solution)/shard_map/while/body/eval_jaxpr/reduce_scatter | solution.py:33
  1510.6 0.7 bitcast_subtract_fusion.3
  1511.3 108.8 %all_gather.11 = f32[1024,128]{1,0:T(8,128)S(1)} all-gather(f32[16,128]{1,0:T(8,128)S(1)} %bitcast_subtract_fusion.3), channel_id=1, replica_groups=mesh['wide'=64,'narrow'=4] {'wide'}, dimensions={0}, use_global_device_ids=true | all-gather | bytes 532480 | tf_op jit(solution)/shard_map/while/body/eval_jaxpr/all_gather | solution.py:41
  1620.1 1.2 fusion.16
  1621.3 9.7 psum.15
  1631.0 0.0 reduce-scatter.5.cloned.1.call-start
  1631.1 2.7 convolution_bitcast_fusion.2
  1633.8 0.0 reduce-scatter.5.cloned.1.call-update
  1633.9 407.3 %reduce-scatter.5.cloned.1.call-done = f32[16,128]{1,0:T(8,128)} async-done(((f32[1024,128]{1,0:T(8,128)}), f32[16,128]{1,0:T(8,128)}) %reduce-scatter.5.cloned.1.call-update) | async-done | bytes 8208 | tf_op jit(solution)/shard_map/while/body/eval_jaxpr/reduce_scatter | solution.py:33
  2041.2 0.7 bitcast_subtract_fusion.3
  2041.9 108.8 %all_gather.11 = f32[1024,128]{1,0:T(8,128)S(1)} all-gather(f32[16,128]{1,0:T(8,128)S(1)} %bitcast_subtract_fusion.3), channel_id=1, replica_groups=mesh['wide'=64,'narrow'=4] {'wide'}, dimensions={0}, use_global_device_ids=true | all-gather | bytes 532480 | tf_op jit(solution)/shard_map/while/body/eval_jaxpr/all_gather | solution.py:41
  2150.7 1.2 fusion.16
  2151.9 9.7 psum.15
  2161.6 0.6 dynamic-slice_bitcast_fusion
  (5 shorter events, 0.0 us)
Async XLA Ops:
  6.5 26.5 %reduce-scatter.3.cloned.1.call-start = ((), (), s32[]{:S(2)}) async-start(), calls=%async_computation.2 | async-start | bytes 40960 | tf_op jit(solution)/shard_map/reduce_scatter | solution.py:21
  7.3 25.7 %copy-start = (f32[1,1,16,128]{3,2,1,0:T(8,128)S(1)}, f32[1,1,16,128]{3,2,1,0:T(8,128)}, u32[]{:S(2)}) copy-start(f32[1,1,16,128]{3,2,1,0:T(8,128)} %param.7) | copy-start | bytes 24580
  33.7 415.5 %reduce-scatter.5.cloned.1.call-start = ((), (), s32[]{:S(2)}) async-start(), calls=%async_computation.3 | async-start | bytes 532480 | tf_op jit(solution)/shard_map/while/body/eval_jaxpr/reduce_scatter | solution.py:33
  568.8 411.3 %reduce-scatter.5.cloned.1.call-start = ((), (), s32[]{:S(2)}) async-start(), calls=%async_computation.3 | async-start | bytes 532480 | tf_op jit(solution)/shard_map/while/body/eval_jaxpr/reduce_scatter | solution.py:33
  1100.5 410.1 %reduce-scatter.5.cloned.1.call-start = ((), (), s32[]{:S(2)}) async-start(), calls=%async_computation.3 | async-start | bytes 532480 | tf_op jit(solution)/shard_map/while/body/eval_jaxpr/reduce_scatter | solution.py:33
  1631.0 410.1 %reduce-scatter.5.cloned.1.call-start = ((), (), s32[]{:S(2)}) async-start(), calls=%async_computation.3 | async-start | bytes 532480 | tf_op jit(solution)/shard_map/while/body/eval_jaxpr/reduce_scatter | solution.py:33
Sparse Core Ops, SparseCore 0:
  9.8 23.1 reduce-scatter.2
  37.2 411.9 reduce-scatter.4
  572.2 407.7 reduce-scatter.4
  1103.7 406.9 reduce-scatter.4
  1634.2 406.9 reduce-scatter.4
where the time goes:
time: 2170 us
  waiting for transfers between devices  1660 us (76%)
  blocking collectives  473 us (22%)
    reduce_scatter x4, waiting for transfers between devices, advance(): lax.psum_scatter(jnp.einsum('cqr,cqk->rk', rows_here, solved, precision=l...  1640 us
    all_gather x4, blocking collectives, advance(): residual_full = lax.all_gather(residual_part, 'wide', axis=0, tiled=True)  435 us
  transfers between devices with their start and end apart: 5, of which 5 were waited for; matrix products, arithmetic and copies ran while one was open for 0% of the time, Pallas kernels for 0%

commit v1 on v0

v1 whole, which is shorter than its diff:
```python
import jax
import jax.numpy as jnp
from jax import lax
from jax.experimental import pallas as pl
from jax.experimental.pallas import tpu as pltpu
from jax.sharding import PartitionSpec as P

MESH = pl.DeviceIdType.MESH
F32, BF16 = jnp.float32, jnp.bfloat16


def kernel(inv_ref, fac_ref, load_ref, child_ref, out_ref,
           kid_v, load_v, stage, staged, p0_buf, p1_src, p1_buf, g_all,
           x_src, x_buf, y_src, y_buf, inv_buf, w_inv, l_buf, w_l, y_hl,
           spread, o_src, o_buf, f_buf,
           loc_sem, p0_sem, p1_sem, x_sem, y_sem, i1_sem, i2_s, i2_r, l1_s, l1_r, l2_s, l2_r,
           o_s, o_r):
    w = lax.axis_index("wide")
    n = lax.axis_index("narrow")
    c = lax.rem(w, 2)
    y = lax.rem(w // 2, 4)
    x = lax.rem(w // 8, 4)
    zh = w // 32
    z = zh * 4 + n
    yc = y * 2 + c

    def dev(zh_, x_, y_, c_, n_):
        return {"wide": ((zh_ * 4 + x_) * 4 + y_) * 2 + c_, "narrow": n_}

    def zdev(z_):
        return dev(z_ // 4, x, y, c, lax.rem(z_, 4))

    def send(src, dst, s_sem, r_sem, to):
        pltpu.make_async_remote_copy(src_ref=src, dst_ref=dst, send_sem=s_sem, recv_sem=r_sem,
                                     device_id=to, device_id_type=MESH).start()

    def settle(like, sem):
        pltpu.make_async_copy(like, like, sem).wait()

    ring = [(2, 0), (2, 1), (1, 0), (1, 1), (3, 0), (3, 1), (0, 1)]

    barrier = pltpu.get_barrier_semaphore()
    for d in (4, 3, 5, 2, 6, 1, 7):
        pl.semaphore_signal(barrier, inc=1, device_id=zdev(lax.rem(z + d, 8)), device_id_type=MESH)
    for d, e in ring:
        pl.semaphore_signal(barrier, inc=1, device_id=dev(zh, x, lax.rem(y + d, 4), lax.rem(c + e, 2), n),
                            device_id_type=MESH)
    for d, e in ring[:-1]:
        pl.semaphore_signal(barrier, inc=1, device_id=dev(zh, lax.rem(x + d, 4), y, lax.rem(c + e, 2), n),
                            device_id_type=MESH)

    kid_in = pltpu.make_async_copy(child_ref, kid_v, loc_sem.at[0])
    load_in = pltpu.make_async_copy(load_ref, load_v, loc_sem.at[1])
    kid_in.start()
    load_in.start()
    own_inv = [pltpu.make_async_copy(inv_ref.at[:, :, pl.ds(pl.multiple_of(h * 512 + x * 128, 128), 128)],
                                     inv_buf.at[:, h, zh * 4 + x], loc_sem.at[2 + h]) for h in range(2)]
    for cp in own_inv:
        cp.start()

    def own_pair(k):
        return (n * (n - 1)) // 2 + k

    def fac_slice(k, x_, c_):
        return fac_ref.at[k, :, pl.ds(pl.multiple_of(c_ * 512 + x_ * 128, 128), 128)]

    def own_fac(k):
        return pltpu.make_async_copy(fac_slice(k, x, c), l_buf.at[own_pair(k), c, zh, x], loc_sem.at[4 + k])

    for k in range(3):
        @pl.when(k < n)
        def _(k=k):
            own_fac(k).start()

    stage[...] = jnp.zeros_like(stage)
    spread[...] = jnp.zeros_like(spread)
    kid_in.wait()
    load_in.wait()

    def window(i):
        return pl.ds(pl.multiple_of(lax.rem(zh * 4 + i + yc, 8) * 16, 16), 16)

    for i in range(4):
        stage[window(i), :] = -kid_v[i]
    stage[window(n), :] = stage[window(n), :] + load_v[...]
    staged[...] = stage[...].T
    p0_buf[z] = staged[pl.ds(pl.multiple_of(z * 16, 16), 16), :]

    pl.semaphore_wait(barrier, 20)

    for d in (4, 3, 5, 2, 6, 1, 7):
        to = lax.rem(z + d, 8)
        send(staged.at[pl.ds(pl.multiple_of(to * 16, 16), 16), :], p0_buf.at[z], p0_sem.at[0], p0_sem.at[1], zdev(to))

    for part in range(2):
        for d in (2, 1, 3):
            xt = lax.rem(x + d, 4)
            for h in range(2):
                cols = pl.ds(pl.multiple_of(h * 512 + xt * 128, 128), 128)
                rows = pl.ds(0, 1) if part == 0 else pl.ds(1, 3)
                send(inv_ref.at[rows, :, cols], inv_buf.at[rows, h, zh * 4 + x], i1_sem.at[0, part], i1_sem.at[1, part],
                     dev(zh, xt, y, c, n))
    for k in range(3):
        @pl.when(k < n)
        def _(k=k):
            for d, e in ring:
                xt, ct = lax.rem(x + d, 4), lax.rem(c + e, 2)
                send(fac_slice(k, xt, ct), l_buf.at[own_pair(k), c, zh, x], l1_s.at[k], l1_r.at[k], dev(zh, xt, y, ct, n))

    def forward_inverse(i):
        mine = inv_buf.at[i, :, pl.ds(pl.multiple_of(zh * 4, 4), 4)]
        for side in range(2):
            @pl.when(n == 3 * side)
            def _():
                for m in range(2):
                    send(mine, mine, i2_s, i2_r.at[i], dev(1 - zh, x, y, c, 2 - 2 * side + m))

    for cp in own_inv:
        cp.wait()
    settle(inv_buf.at[0, :, pl.ds(0, 3)], i1_sem.at[1, 0])
    forward_inverse(0)

    settle(p0_buf.at[pl.ds(0, 7)], p0_sem.at[1])
    own = p0_buf[0]
    for k in range(1, 8):
        own = own + p0_buf[k]
    p1_src[...] = own
    p1_buf[yc] = own
    for d, e in ring:
        send(p1_src, p1_buf.at[yc], p1_sem.at[0], p1_sem.at[1], dev(zh, x, lax.rem(y + d, 4), lax.rem(c + e, 2), n))

    def forward_factor(i):
        @pl.when(n == i)
        def _():
            for k in range(i):
                own_fac(k).wait()
                settle(y_buf.at[0, pl.ds(0, 7)], l1_r.at[k])
                mine = l_buf.at[i * (i - 1) // 2 + k, :, zh]
                for d in (4, 3, 5, 2, 6, 1, 7):
                    send(mine, mine, l2_s.at[k], l2_r.at[i * (i - 1) // 2 + k], zdev(lax.rem(z + d, 8)))

    forward_factor(1)
    settle(inv_buf.at[pl.ds(1, 3), :, pl.ds(0, 3)], i1_sem.at[1, 1])
    forward_inverse(1)

    def split(v):
        hi = v.astype(BF16)
        return hi, (v - hi.astype(F32)).astype(BF16)

    def prepare_inverse(i):
        settle(inv_buf.at[i, :, pl.ds(0, 4)], i2_r.at[i])
        for h in range(2):
            hi, lo = split(inv_buf[i, h].reshape(128, 128))
            w_inv[i, 0:128, h * 128:(h + 1) * 128] = hi
            w_inv[i, 128:256, h * 128:(h + 1) * 128] = lo

    def prepare_factor(i, k):
        pair = i * (i - 1) // 2 + k

        @pl.when(n == i)
        def _():
            settle(l_buf.at[pair, :, 0], l2_r.at[pair])

        @pl.when(n != i)
        def _():
            settle(l_buf.at[pair], l2_r.at[pair])
        hi, lo = split(l_buf[pair].reshape(256, 128))
        w_l[pair, :, 0:128] = hi
        w_l[pair, :, 128:256] = lo

    def fold(d):
        return (d[0:16, 0:128] + d[16:32, 128:256]) + (d[0:16, 128:256] + d[16:32, 0:128])

    def stacked(v):
        hi, lo = split(v)
        return jnp.concatenate([hi, lo], axis=0)

    def apply_inverse(i, r):
        return fold(lax.dot_general(stacked(r), w_inv[i], (((1,), (1,)), ((), ())), preferred_element_type=F32))

    def apply_factor(i, k):
        pair = i * (i - 1) // 2 + k
        return fold(jnp.dot(y_hl[k], w_l[pair], preferred_element_type=F32))

    def spread_cases(piece):
        at = pl.ds(pl.multiple_of(z * 16, 16), 16)
        spread[at, :] = piece
        return spread[...].T

    def send_x(i, partial):
        x_src[i] = partial
        x_buf[i, c * 4 + x] = partial
        for d, e in ring:
            send(x_src.at[i], x_buf.at[i, c * 4 + x], x_sem.at[0, i], x_sem.at[1, i],
                 dev(zh, lax.rem(x + d, 4), y, lax.rem(c + e, 2), n))

    def send_y(i, partial):
        y_src[i] = partial
        y_buf[i, c * 4 + y] = partial
        for d, e in ring:
            send(y_src.at[i], y_buf.at[i, c * 4 + y], y_sem.at[0, i], y_sem.at[1, i],
                 dev(zh, x, lax.rem(y + d, 4), lax.rem(c + e, 2), n))

    def halves(buf, i):
        return [(buf[i, 4 * h] + buf[i, 4 * h + 1]) + (buf[i, 4 * h + 2] + buf[i, 4 * h + 3]) for h in range(2)]

    def solved_parts(i):
        settle(x_buf.at[i, pl.ds(0, 7)], x_sem.at[1, i])
        parts = halves(x_buf, i)
        y_hl[i] = stacked(jnp.concatenate(parts, axis=1))
        return parts

    def send_out(i, parts):
        o_src[i] = spread_cases(jnp.where(c == 0, parts[0], parts[1]))
        for g in range(2):
            rows = o_src.at[i, pl.ds(pl.multiple_of((g * 4 + x) * 16, 16), 16), :]
            own_place = jnp.logical_and(n == i, zh == g)

            @pl.when(own_place)
            def _():
                o_buf[z] = o_src[i, pl.ds(pl.multiple_of((g * 4 + x) * 16, 16), 16), :]

            @pl.when(jnp.logical_not(own_place))
            def _():
                send(rows, o_buf.at[z], o_s.at[i], o_r.at[0], dev(g, x, y, c, i))

    prepare_inverse(0)
    settle(p1_buf.at[pl.ds(0, 7)], p1_sem.at[1])
    lane_window = lax.broadcasted_iota(jnp.int32, (16, 128), 1) // 16

    def gathered(i):
        for h in range(2):
            first = h * 4 + i
            v = p1_buf[0]
            for k in range(1, 8):
                v = jnp.where(lane_window == (first + k) % 8, p1_buf[k], v)
            if first:
                v = pltpu.roll(v, 128 - first * 16, 1)
            g_all[i, :, h * 128:(h + 1) * 128] = v

    gathered(0)
    send_x(0, apply_inverse(0, g_all[0]))
    forward_factor(2)
    forward_inverse(2)
    for i in range(1, 4):
        gathered(i)
    prepare_factor(1, 0)
    parts = solved_parts(0)

    for i in range(1, 4):
        ahead = None
        for k in range(i - 1):
            term = apply_factor(i, k)
            ahead = term if ahead is None else ahead + term
        last = apply_factor(i, i - 1)
        send_y(i - 1, last if ahead is None else ahead + last)
        send_out(i - 1, parts)
        prepare_inverse(i)
        if i == 1:
            forward_factor(3)
            forward_inverse(3)
        if i < 3:
            for k in range(i + 1):
                prepare_factor(i + 1, k)
        settle(y_buf.at[i - 1, pl.ds(0, 7)], y_sem.at[1, i - 1])
        sums = halves(y_buf, i - 1)
        partial = apply_inverse(i, g_all[i] - jnp.concatenate(sums, axis=1))
        if i < 3:
            send_x(i, partial)
            parts = solved_parts(i)

    o_src[3] = spread_cases(partial)
    for g in range(2):
        for d in (2, 1, 3, 0):
            xt = lax.rem(x + d, 4)
            at = pl.ds(pl.multiple_of((g * 4 + xt) * 16, 16), 16)
            if d:
                send(o_src.at[3, at, :], f_buf.at[z * 4 + x], o_s.at[3], o_r.at[1], dev(g, xt, y, c, 3))
            else:
                own_place = jnp.logical_and(n == 3, zh == g)

                @pl.when(own_place)
                def _():
                    f_buf[z * 4 + x] = o_src[3, at, :]

                @pl.when(jnp.logical_not(own_place))
                def _():
                    send(o_src.at[3, at, :], f_buf.at[z * 4 + x], o_s.at[3], o_r.at[1], dev(g, xt, y, c, 3))

    settle(p0_buf.at[pl.ds(0, 7)], p0_sem.at[0])
    settle(p1_buf.at[pl.ds(0, 7)], p1_sem.at[0])
    for i in range(3):
        settle(x_buf.at[i, pl.ds(0, 7)], x_sem.at[0, i])
        settle(y_buf.at[i, pl.ds(0, 7)], y_sem.at[0, i])
    settle(inv_buf.at[0, :, pl.ds(0, 3)], i1_sem.at[0, 0])
    settle(inv_buf.at[pl.ds(1, 3), :, pl.ds(0, 3)], i1_sem.at[0, 1])

    @pl.when(jnp.logical_or(n == 0, n == 3))
    def _():
        settle(inv_buf, i2_s)

    for k in range(3):
        @pl.when(k < n)
        def _(k=k):
            settle(y_buf.at[0, pl.ds(0, 7)], l1_s.at[k])
            settle(inv_buf.at[:, :, pl.ds(0, 7)], l2_s.at[k])

    for i in range(4):
        count = 2 if i < 3 else 8

        @pl.when(n == i)
        def _(i=i, count=count):
            settle(f_buf.at[pl.ds(0, count - 1)], o_s.at[i])

        @pl.when(n != i)
        def _(i=i, count=count):
            settle(f_buf.at[pl.ds(0, count)], o_s.at[i])

    @pl.when(n < 3)
    def _():
        settle(o_buf.at[pl.ds(0, 7)], o_r.at[0])
        total = o_buf[0]
        for k in range(1, 8):
            total = total + o_buf[k]
        out_ref[...] = total

    @pl.when(n == 3)
    def _():
        settle(f_buf.at[pl.ds(0, 31)], o_r.at[1])
        total = f_buf[0]
        for k in range(1, 32):
            total = total + f_buf[k]
        out_ref[...] = total


def body(factor_rows, load_vectors, child_updates, block_inverses):
    dma = pltpu.SemaphoreType.DMA
    out = pl.pallas_call(
        kernel,
        out_shape=jax.ShapeDtypeStruct((16, 128), F32),
        in_specs=[pl.BlockSpec(memory_space=pl.ANY)] * 4,
        out_specs=pl.BlockSpec(memory_space=pltpu.VMEM),
        scratch_shapes=[
            pltpu.VMEM((4, 16, 128), F32), pltpu.VMEM((16, 128), F32),
            pltpu.VMEM((128, 128), F32), pltpu.VMEM((128, 128), F32),
            pltpu.VMEM((8, 16, 128), F32), pltpu.VMEM((16, 128), F32), pltpu.VMEM((8, 16, 128), F32),
            pltpu.VMEM((4, 16, 256), F32),
            pltpu.VMEM((3, 16, 128), F32), pltpu.VMEM((3, 8, 16, 128), F32),
            pltpu.VMEM((3, 16, 128), F32), pltpu.VMEM((3, 8, 16, 128), F32),
            pltpu.VMEM((4, 2, 8, 16, 128), F32), pltpu.VMEM((4, 256, 256), BF16),
            pltpu.VMEM((6, 2, 2, 4, 16, 128), F32), pltpu.VMEM((6, 256, 256), BF16),
            pltpu.VMEM((3, 32, 256), BF16),
            pltpu.VMEM((128, 128), F32), pltpu.VMEM((4, 128, 128), F32),
            pltpu.VMEM((8, 16, 128), F32), pltpu.VMEM((32, 16, 128), F32),
            dma((7,)), dma((2,)), dma((2,)), dma((2, 3)), dma((2, 3)), dma((2, 2)),
            dma, dma((4,)), dma((3,)), dma((3,)), dma((3,)), dma((6,)), dma((4,)), dma((2,)),
        ],
        compiler_params=pltpu.CompilerParams(collective_id=0, has_side_effects=True, vmem_limit_bytes=24 << 20),
        name="substitution",
    )(
        block_inverses,
        factor_rows.reshape(4, 16, 1024),
        load_vectors.reshape(16, 128),
        child_updates.reshape(4, 16, 128),
    )
    return out.reshape(1, 1, 16, 128)


def solution(mesh):
    placed = (
        P(None, "narrow", None, "wide", None, None),
        P(None, "narrow", "wide", None),
        P("narrow", None, None, "wide", None),
        P(None, "wide", None),
    )
    return jax.shard_map(
        body, mesh=mesh, in_specs=placed, out_specs=P(None, "narrow", "wide", None), check_vma=False
    )
```

time: 2170 us -> 64 us (0.03)
  waiting for transfers between devices: 1660 us -> 0 us
  blocking collectives: 473 us -> 0 us
  Pallas kernels: 0 us -> 59.8 us
    reduce_scatter x5 -> x0, waiting for transfers between devices: 1660 us -> none  [the longest x4 1640 us: advance(): lax.psum_scatter(jnp.einsum('cqr,cqk->rk', rows_here, solved, precision=l...]
    all_gather x4 -> x0, blocking collectives: 435 us -> none  [advance(): residual_full = lax.all_gather(residual_part, 'wide', axis=0, tiled=True)]
    pallas_call x0 -> x1, Pallas kernels: none -> 59.8 us  [body(): pl.pallas_call(kernel, out_shape=jax.ShapeDtypeStruct((16, 128), F32), in...]
    psum x4 -> x0, blocking collectives: 37.8 us -> none  [from_root(): return lax.psum(jnp.where(mine, shard, jnp.zeros_like(shard)), axis)]
  transfers between devices with their start and end apart: 5 -> 0, of which waited for: 5 -> 0; matrix products, arithmetic and copies ran while one was open for 0% -> 0% of each run, Pallas kernels for 0% -> 0%
where the time goes in v1:
time: 64 us; the launch traced here: 63.8 us
  Pallas kernels  59.8 us (93%)
  local copies, waits for them, and re-layouts  3.95 us (6%)
    pallas_call x1, Pallas kernels, body(): pl.pallas_call(kernel, out_shape=jax.ShapeDtypeStruct((16, 128), F32), in...  59.8 us
    unnamed x9, local copies, waits for them, and re-layouts  3.95 us

profile of v1, /device:TPU:96, one launch (start us, length us, event | category | flops | bytes accessed | tf_op | source)
XLA Modules:
  0.0 63.8 jit_solution(7744569274261123570)
XLA Ops:
  0.0 0.0 copy-start
  0.0 0.9 %copy-done = f32[4,16,1024]{2,1,0:T(8,128)S(1)} copy-done((f32[4,16,1024]{2,1,0:T(8,128)S(1)}, f32[4,16,1024]{2,1,0:T(8,128)}, u32[]{:S(2)}) %copy-start) | copy-done | bytes 262168
  1.0 0.0 copy-start.1
  1.0 0.9 %copy-done.1 = f32[1,1,4,1,16,1024]{5,4,3,2,1,0:T(8,128)S(1)} copy-done((f32[1,1,4,1,16,1024]{5,4,3,2,1,0:T(8,128)S(1)}, f32[1,1,4,1,16,1024]{5,4,3,2,1,0:T(8,128)}, u32[]{:S(2)}) %copy-start.1) | copy-done | bytes 262168
  1.9 0.0 copy-start.2
  1.9 0.8 %copy-done.2 = f32[1,1,4,16,128]{4,3,2,1,0:T(8,128)S(1)} copy-done((f32[1,1,4,16,128]{4,3,2,1,0:T(8,128)S(1)}, f32[1,1,4,16,128]{4,3,2,1,0:T(8,128)}, u32[]{:S(2)}) %copy-start.2) | copy-done | bytes 32792
  2.7 0.0 copy-start.3
  2.7 0.7 %copy-done.3 = f32[1,1,16,128]{3,2,1,0:T(8,128)S(1)} copy-done((f32[1,1,16,128]{3,2,1,0:T(8,128)S(1)}, f32[1,1,16,128]{3,2,1,0:T(8,128)}, u32[]{:S(2)}) %copy-start.3) | copy-done | bytes 8216
  3.4 59.8 %substitution.1 = f32[16,128]{1,0:T(8,128)S(1)} custom-call(f32[4,16,1024]{2,1,0:T(8,128)S(1)} %copy-done, f32[4,16,1024]{2,1,0:T(8,128)S(1)} %bitcast.4, f32[16,128]{1,0:T(8,128)S(1)} %bitcast.7, f32[4,16,128]{2,1,0:T(8,128)S(1)} %bitcast.6), custom_call_target="tpu_custom_call" | custom-call | tf_op jit(solution)/shard_map/substitution/pallas_call | solution.py:338
  63.2 0.6 copy.6
Async XLA Ops:
  0.0 0.9 %copy-start = (f32[4,16,1024]{2,1,0:T(8,128)S(1)}, f32[4,16,1024]{2,1,0:T(8,128)}, u32[]{:S(2)}) copy-start(f32[4,16,1024]{2,1,0:T(8,128)} %inv_ref.1) | copy-start | bytes 786436
  1.0 0.9 %copy-start.1 = (f32[1,1,4,1,16,1024]{5,4,3,2,1,0:T(8,128)S(1)}, f32[1,1,4,1,16,1024]{5,4,3,2,1,0:T(8,128)}, u32[]{:S(2)}) copy-start(f32[1,1,4,1,16,1024]{5,4,3,2,1,0:T(8,128)} %param.4) | copy-start | bytes 786436
  1.9 0.8 %copy-start.2 = (f32[1,1,4,16,128]{4,3,2,1,0:T(8,128)S(1)}, f32[1,1,4,16,128]{4,3,2,1,0:T(8,128)}, u32[]{:S(2)}) copy-start(f32[1,1,4,16,128]{4,3,2,1,0:T(8,128)} %param.6) | copy-start | bytes 98308
  2.7 0.7 %copy-start.3 = (f32[1,1,16,128]{3,2,1,0:T(8,128)S(1)}, f32[1,1,16,128]{3,2,1,0:T(8,128)}, u32[]{:S(2)}) copy-start(f32[1,1,16,128]{3,2,1,0:T(8,128)} %param.5) | copy-start | bytes 24580

commit v2 on v1

--- a/solution.py
+++ b/solution.py
@@ -13,7 +13,7 @@
            kid_v, load_v, stage, staged, p0_buf, p1_src, p1_buf, g_all,
            x_src, x_buf, y_src, y_buf, inv_buf, w_inv, l_buf, w_l, y_hl,
            spread, o_src, o_buf, f_buf,
-           loc_sem, p0_sem, p1_sem, x_sem, y_sem, i1_sem, i2_s, i2_r, l1_s, l1_r, l2_s, l2_r,
+           loc_sem, p0_sem, p1_sem, x_sem, y_sem, i1_sem, i2_s, i2_r, l1_s, l1_r, l2_s, l2_r, l3_s,
            o_s, o_r):
     w = lax.axis_index("wide")
     n = lax.axis_index("narrow")
@@ -92,33 +92,51 @@
         to = lax.rem(z + d, 8)
         send(staged.at[pl.ds(pl.multiple_of(to * 16, 16), 16), :], p0_buf.at[z], p0_sem.at[0], p0_sem.at[1], zdev(to))
 
-    for part in range(2):
-        for d in (2, 1, 3):
-            xt = lax.rem(x + d, 4)
-            for h in range(2):
-                cols = pl.ds(pl.multiple_of(h * 512 + xt * 128, 128), 128)
-                rows = pl.ds(0, 1) if part == 0 else pl.ds(1, 3)
-                send(inv_ref.at[rows, :, cols], inv_buf.at[rows, h, zh * 4 + x], i1_sem.at[0, part], i1_sem.at[1, part],
-                     dev(zh, xt, y, c, n))
-    for k in range(3):
-        @pl.when(k < n)
-        def _(k=k):
-            for d, e in ring:
-                xt, ct = lax.rem(x + d, 4), lax.rem(c + e, 2)
-                send(fac_slice(k, xt, ct), l_buf.at[own_pair(k), c, zh, x], l1_s.at[k], l1_r.at[k], dev(zh, xt, y, ct, n))
-
-    def forward_inverse(i):
+    def start_weights():
+        for part in range(2):
+            for d in (2, 1, 3):
+                xt = lax.rem(x + d, 4)
+                for h in range(2):
+                    cols = pl.ds(pl.multiple_of(h * 512 + xt * 128, 128), 128)
+                    rows = pl.ds(0, 1) if part == 0 else pl.ds(1, 3)
+                    send(inv_ref.at[rows, :, cols], inv_buf.at[rows, h, zh * 4 + x], i1_sem.at[0, part], i1_sem.at[1, part],
+                         dev(zh, xt, y, c, n))
+        for k in range(3):
+            @pl.when(k < n)
+            def _(k=k):
+                for d, e in ring:
+                    xt, ct = lax.rem(x + d, 4), lax.rem(c + e, 2)
+                    send(fac_slice(k, xt, ct), l_buf.at[own_pair(k), c, zh, x], l1_s.at[k], l1_r.at[k], dev(zh, xt, y, ct, n))
+
+    start_weights()
+
+    def arrived_inverse(part):
+        settle(inv_buf.at[pl.ds(part, 1 + 2 * part), :, pl.ds(0, 3)], i1_sem.at[1, part])
+
+    def forward_inverse(i, both):
         mine = inv_buf.at[i, :, pl.ds(pl.multiple_of(zh * 4, 4), 4)]
         for side in range(2):
             @pl.when(n == 3 * side)
-            def _():
-                for m in range(2):
-                    send(mine, mine, i2_s, i2_r.at[i], dev(1 - zh, x, y, c, 2 - 2 * side + m))
+            def _(side=side):
+                send(mine, mine, i2_s, i2_r.at[i], dev(1 - zh, x, y, c, 3 - 3 * side))
+                if both:
+                    send(mine, mine, i2_s, i2_r.at[i], dev(1 - zh, x, y, c, 2 - side))
+
+    def relay_inverse(i):
+        other = inv_buf.at[i, :, pl.ds(pl.multiple_of(4 - zh * 4, 4), 4)]
+
+        @pl.when(jnp.logical_or(n == 0, n == 3))
+        def _():
+            settle(inv_buf.at[i, :, pl.ds(0, 4)], i2_r.at[i])
+        for side in range(2):
+            @pl.when(n == 3 * side)
+            def _(side=side):
+                send(other, other, i2_s, i2_r.at[i], dev(zh, x, y, c, 1 + side))
 
     for cp in own_inv:
         cp.wait()
-    settle(inv_buf.at[0, :, pl.ds(0, 3)], i1_sem.at[1, 0])
-    forward_inverse(0)
+    arrived_inverse(0)
+    forward_inverse(0, True)
 
     settle(p0_buf.at[pl.ds(0, 7)], p0_sem.at[1])
     own = p0_buf[0]
@@ -136,19 +154,40 @@
                 own_fac(k).wait()
                 settle(y_buf.at[0, pl.ds(0, 7)], l1_r.at[k])
                 mine = l_buf.at[i * (i - 1) // 2 + k, :, zh]
-                for d in (4, 3, 5, 2, 6, 1, 7):
+                for d in (2, 6, 1, 7):
                     send(mine, mine, l2_s.at[k], l2_r.at[i * (i - 1) // 2 + k], zdev(lax.rem(z + d, 8)))
 
+    def relay_factor(i):
+        @pl.when(n == (i + 2) % 4)
+        def _():
+            for k in range(i):
+                pair = i * (i - 1) // 2 + k
+                settle(l_buf.at[pair], l2_r.at[pair])
+                for d in (1, 7):
+                    origin = lax.rem(z + (6 if d == 1 else 2), 8) // 4
+                    held = l_buf.at[pair, :, origin]
+                    send(held, held, l3_s.at[k], l2_r.at[pair], zdev(lax.rem(z + d, 8)))
+
+                    @pl.when(c == d // 7)
+                    def _(d=d, held=held):
+                        send(held, held, l3_s.at[k], l2_r.at[pair], zdev(lax.rem(z + (2 if d == 1 else 6), 8)))
+
     forward_factor(1)
-    settle(inv_buf.at[pl.ds(1, 3), :, pl.ds(0, 3)], i1_sem.at[1, 1])
-    forward_inverse(1)
+    forward_factor(2)
+    arrived_inverse(1)
+    forward_inverse(1, False)
 
     def split(v):
         hi = v.astype(BF16)
         return hi, (v - hi.astype(F32)).astype(BF16)
 
     def prepare_inverse(i):
-        settle(inv_buf.at[i, :, pl.ds(0, 4)], i2_r.at[i])
+        if i == 0:
+            settle(inv_buf.at[i, :, pl.ds(0, 4)], i2_r.at[i])
+        else:
+            @pl.when(jnp.logical_and(n != 0, n != 3))
+            def _():
+                settle(inv_buf.at[i, :, pl.ds(0, 4)], i2_r.at[i])
         for h in range(2):
             hi, lo = split(inv_buf[i, h].reshape(128, 128))
             w_inv[i, 0:128, h * 128:(h + 1) * 128] = hi
@@ -161,7 +200,7 @@
         def _():
             settle(l_buf.at[pair, :, 0], l2_r.at[pair])
 
-        @pl.when(n != i)
+        @pl.when(jnp.logical_and(n != i, n != (i + 2) % 4))
         def _():
             settle(l_buf.at[pair], l2_r.at[pair])
         hi, lo = split(l_buf[pair].reshape(256, 128))
@@ -240,8 +279,9 @@
 
     gathered(0)
     send_x(0, apply_inverse(0, g_all[0]))
-    forward_factor(2)
-    forward_inverse(2)
+    relay_factor(1)
+    forward_factor(3)
+    relay_inverse(1)
     for i in range(1, 4):
         gathered(i)
     prepare_factor(1, 0)
@@ -255,18 +295,21 @@
         last = apply_factor(i, i - 1)
         send_y(i - 1, last if ahead is None else ahead + last)
         send_out(i - 1, parts)
+        if i == 1:
+            relay_factor(2)
+        if i < 3:
+            forward_inverse(i + 1, False)
         prepare_inverse(i)
-        if i == 1:
-            forward_factor(3)
-            forward_inverse(3)
-        if i < 3:
-            for k in range(i + 1):
-                prepare_factor(i + 1, k)
         settle(y_buf.at[i - 1, pl.ds(0, 7)], y_sem.at[1, i - 1])
         sums = halves(y_buf, i - 1)
         partial = apply_inverse(i, g_all[i] - jnp.concatenate(sums, axis=1))
         if i < 3:
             send_x(i, partial)
+            relay_inverse(i + 1)
+            if i == 1:
+                relay_factor(3)
+            for k in range(i + 1):
+                prepare_factor(i + 1, k)
             parts = solved_parts(i)
 
     o_src[3] = spread_cases(partial)
@@ -287,23 +330,30 @@
                 def _():
                     send(o_src.at[3, at, :], f_buf.at[z * 4 + x], o_s.at[3], o_r.at[1], dev(g, xt, y, c, 3))
 
+    def drain_weights():
+        settle(inv_buf.at[0, :, pl.ds(0, 3)], i1_sem.at[0, 0])
+        settle(inv_buf.at[pl.ds(1, 3), :, pl.ds(0, 3)], i1_sem.at[0, 1])
+
+        @pl.when(jnp.logical_or(n == 0, n == 3))
+        def _():
+            settle(inv_buf, i2_s)
+
+        for k in range(3):
+            @pl.when(k < n)
+            def _(k=k):
+                settle(y_buf.at[0, pl.ds(0, 7)], l1_s.at[k])
+                settle(l_buf.at[pl.ds(0, 2)], l2_s.at[k])
+
+            @pl.when(k < lax.rem(n + 2, 4))
+            def _(k=k):
+                settle(inv_buf.at[:, :, pl.ds(0, 3)], l3_s.at[k])
+
+    drain_weights()
     settle(p0_buf.at[pl.ds(0, 7)], p0_sem.at[0])
     settle(p1_buf.at[pl.ds(0, 7)], p1_sem.at[0])
     for i in range(3):
         settle(x_buf.at[i, pl.ds(0, 7)], x_sem.at[0, i])
         settle(y_buf.at[i, pl.ds(0, 7)], y_sem.at[0, i])
-    settle(inv_buf.at[0, :, pl.ds(0, 3)], i1_sem.at[0, 0])
-    settle(inv_buf.at[pl.ds(1, 3), :, pl.ds(0, 3)], i1_sem.at[0, 1])
-
-    @pl.when(jnp.logical_or(n == 0, n == 3))
-    def _():
-        settle(inv_buf, i2_s)
-
-    for k in range(3):
-        @pl.when(k < n)
-        def _(k=k):
-            settle(y_buf.at[0, pl.ds(0, 7)], l1_s.at[k])
-            settle(inv_buf.at[:, :, pl.ds(0, 7)], l2_s.at[k])
 
     for i in range(4):
         count = 2 if i < 3 else 8
@@ -338,7 +388,7 @@
     out = pl.pallas_call(
         kernel,
         out_shape=jax.ShapeDtypeStruct((16, 128), F32),
-        in_specs=[pl.BlockSpec(memory_space=pl.ANY)] * 4,
+        in_specs=[pl.BlockSpec(memory_space=pltpu.HBM)] * 4,
         out_specs=pl.BlockSpec(memory_space=pltpu.VMEM),
         scratch_shapes=[
             pltpu.VMEM((4, 16, 128), F32), pltpu.VMEM((16, 128), F32),
@@ -353,9 +403,9 @@
             pltpu.VMEM((128, 128), F32), pltpu.VMEM((4, 128, 128), F32),
             pltpu.VMEM((8, 16, 128), F32), pltpu.VMEM((32, 16, 128), F32),
             dma((7,)), dma((2,)), dma((2,)), dma((2, 3)), dma((2, 3)), dma((2, 2)),
-            dma, dma((4,)), dma((3,)), dma((3,)), dma((3,)), dma((6,)), dma((4,)), dma((2,)),
+            dma, dma((4,)), dma((3,)), dma((3,)), dma((3,)), dma((6,)), dma((3,)), dma((4,)), dma((2,)),
         ],
-        compiler_params=pltpu.CompilerParams(collective_id=0, has_side_effects=True, vmem_limit_bytes=24 << 20),
+        compiler_params=pltpu.CompilerParams(collective_id=0, has_side_effects=True, vmem_limit_bytes=60 << 20),
         name="substitution",
     )(
         block_inverses,

time: 64 us -> 56.1 us (0.88)
  Pallas kernels: 59.8 us -> 54.6 us
  local copies, waits for them, and re-layouts: 3.95 us -> 1.3 us
    pallas_call x1, Pallas kernels: 59.8 us -> 54.6 us  [body(): pl.pallas_call(kernel, out_shape=jax.ShapeDtypeStruct((16, 128), F32), in...]
    unnamed x9 -> x1, local copies, waits for them, and re-layouts: 3.95 us -> 1.3 us
where the time goes in v2:
time: 56.1 us; the launch traced here: 56 us
  Pallas kernels  54.6 us (97%)
  local copies, waits for them, and re-layouts  1.3 us (2%)
    pallas_call x1, Pallas kernels, body(): pl.pallas_call(kernel, out_shape=jax.ShapeDtypeStruct((16, 128), F32), in...  54.6 us
    unnamed x1, local copies, waits for them, and re-layouts  1.3 us

profile of v2, /device:TPU:96, one launch (start us, length us, event | category | flops | bytes accessed | tf_op | source)
XLA Modules:
  0.0 56.0 jit_solution(17181430869217594705)
XLA Ops:
  0.0 54.6 %substitution.1 = f32[16,128]{1,0:T(8,128)} custom-call(f32[4,16,1024]{2,1,0:T(8,128)} %inv_ref.1, f32[4,16,1024]{2,1,0:T(8,128)} %bitcast.4, f32[16,128]{1,0:T(8,128)} %bitcast.7, f32[4,16,128]{2,1,0:T(8,128)} %bitcast.6), custom_call_target="tpu_custom_call" | custom-call | tf_op jit(solution)/shard_map/substitution/pallas_call | solution.py:388
  54.7 1.3 %copy.6 = f32[1,1,16,128]{3,2,1,0:T(8,128)} copy(f32[1,1,16,128]{3,2,1,0:T(8,128)} %bitcast.5) | data formatting | bytes 16384

commit v3 on v2

--- a/solution.py
+++ b/solution.py
@@ -8,12 +8,29 @@
 MESH = pl.DeviceIdType.MESH
 F32, BF16 = jnp.float32, jnp.bfloat16
 
+PLAN = {
+    "gather": [("f", 1), ("f", 2), ("s", 1), ("d", 1, False)],
+    "gather end": [],
+    "x0": [("f", 3)],
+    "x0 end": [("a", 1), ("j", 1)],
+    "y0": [("r", 2), ("i", 2, False)],
+    "y0 end": [],
+    "x1": [],
+    "x1 end": [("j", 2), ("m",), ("r", 3)],
+    "y1": [("i", 3, False)],
+    "y1 end": [],
+    "x2": [],
+    "x2 end": [("j", 3)],
+    "y2": [],
+    "y2 end": [],
+}
+
 
 def kernel(inv_ref, fac_ref, load_ref, child_ref, out_ref,
            kid_v, load_v, stage, staged, p0_buf, p1_src, p1_buf, g_all,
            x_src, x_buf, y_src, y_buf, inv_buf, w_inv, l_buf, w_l, y_hl,
-           spread, o_src, o_buf, f_buf,
-           loc_sem, p0_sem, p1_sem, x_sem, y_sem, i1_sem, i2_s, i2_r, l1_s, l1_r, l2_s, l2_r, l3_s,
+           spread, o_src, o_buf, f_buf, f_src, away_src, away_buf, back_src, back_buf,
+           loc_sem, p0_sem, p1_sem, x_sem, y_sem, i1_sem, i2_s, i2_r, l1_s, l1_r, l2_s, l2_r, l3_s, away_sem, back_sem,
            o_s, o_r):
     w = lax.axis_index("wide")
     n = lax.axis_index("narrow")
@@ -49,6 +66,11 @@
         pl.semaphore_signal(barrier, inc=1, device_id=dev(zh, lax.rem(x + d, 4), y, lax.rem(c + e, 2), n),
                             device_id_type=MESH)
 
+    near = jnp.where(n < 2, 3, 0)
+    for d in (2, 1, 3):
+        pl.semaphore_signal(barrier, inc=1, device_id=dev(1 - zh, lax.rem(x + d, 4), y, c, near), device_id_type=MESH)
+    at_end = jnp.logical_or(n == 0, n == 3)
+
     kid_in = pltpu.make_async_copy(child_ref, kid_v, loc_sem.at[0])
     load_in = pltpu.make_async_copy(load_ref, load_v, loc_sem.at[1])
     kid_in.start()
@@ -86,29 +108,51 @@
     staged[...] = stage[...].T
     p0_buf[z] = staged[pl.ds(pl.multiple_of(z * 16, 16), 16), :]
 
-    pl.semaphore_wait(barrier, 20)
+    @pl.when(at_end)
+    def _():
+        pl.semaphore_wait(barrier, 26)
+
+    @pl.when(jnp.logical_not(at_end))
+    def _():
+        pl.semaphore_wait(barrier, 20)
 
     for d in (4, 3, 5, 2, 6, 1, 7):
         to = lax.rem(z + d, 8)
         send(staged.at[pl.ds(pl.multiple_of(to * 16, 16), 16), :], p0_buf.at[z], p0_sem.at[0], p0_sem.at[1], zdev(to))
 
-    def start_weights():
-        for part in range(2):
-            for d in (2, 1, 3):
-                xt = lax.rem(x + d, 4)
-                for h in range(2):
-                    cols = pl.ds(pl.multiple_of(h * 512 + xt * 128, 128), 128)
-                    rows = pl.ds(0, 1) if part == 0 else pl.ds(1, 3)
-                    send(inv_ref.at[rows, :, cols], inv_buf.at[rows, h, zh * 4 + x], i1_sem.at[0, part], i1_sem.at[1, part],
-                         dev(zh, xt, y, c, n))
+    def start_inverse(part):
+        for d in (2, 1, 3):
+            xt = lax.rem(x + d, 4)
+            for h in range(2):
+                cols = pl.ds(pl.multiple_of(h * 512 + xt * 128, 128), 128)
+                rows = pl.ds(0, 1) if part == 0 else pl.ds(1, 3)
+                send(inv_ref.at[rows, :, cols], inv_buf.at[rows, h, zh * 4 + x], i1_sem.at[0, part], i1_sem.at[1, part],
+                     dev(zh, xt, y, c, n))
+
+    def start_factor():
         for k in range(3):
             @pl.when(k < n)
             def _(k=k):
                 for d, e in ring:
                     xt, ct = lax.rem(x + d, 4), lax.rem(c + e, 2)
-                    send(fac_slice(k, xt, ct), l_buf.at[own_pair(k), c, zh, x], l1_s.at[k], l1_r.at[k], dev(zh, xt, y, ct, n))
-
-    start_weights()
+                    send(fac_slice(k, xt, ct), l_buf.at[own_pair(k), c, zh, x], l1_s.at[k], l1_r.at[k],
+                         dev(zh, xt, y, ct, n))
+
+    def direct_inverse(i, both):
+        for side in range(2):
+            @pl.when(n == 3 * side)
+            def _(side=side):
+                for d in (2, 1, 3, 0):
+                    xt = lax.rem(x + d, 4)
+                    for h in range(2):
+                        cols = pl.ds(pl.multiple_of(h * 512 + xt * 128, 128), 128)
+                        for lane in ((3 - 3 * side, 2 - side) if both else (3 - 3 * side,)):
+                            send(inv_ref.at[i, :, cols], inv_buf.at[i, h, zh * 4 + x], i2_s, i2_r.at[i],
+                                 dev(1 - zh, xt, y, c, lane))
+
+    direct_inverse(0, True)
+    start_inverse(0)
+    start_factor()
 
     def arrived_inverse(part):
         settle(inv_buf.at[pl.ds(part, 1 + 2 * part), :, pl.ds(0, 3)], i1_sem.at[1, part])
@@ -136,7 +180,6 @@
     for cp in own_inv:
         cp.wait()
     arrived_inverse(0)
-    forward_inverse(0, True)
 
     settle(p0_buf.at[pl.ds(0, 7)], p0_sem.at[1])
     own = p0_buf[0]
@@ -150,32 +193,81 @@
     def forward_factor(i):
         @pl.when(n == i)
         def _():
-            for k in range(i):
+            own = range(1, 3) if i == 3 else range(i)
+            for k in own:
                 own_fac(k).wait()
                 settle(y_buf.at[0, pl.ds(0, 7)], l1_r.at[k])
-                mine = l_buf.at[i * (i - 1) // 2 + k, :, zh]
-                for d in (2, 6, 1, 7):
-                    send(mine, mine, l2_s.at[k], l2_r.at[i * (i - 1) // 2 + k], zdev(lax.rem(z + d, 8)))
+            for ds in (((4, 3, 5, 2, 6, 1, 7),) if i == 1 else ((2, 6), (1, 7))):
+                for k in own:
+                    pair = i * (i - 1) // 2 + k
+                    mine = l_buf.at[pair, :, zh]
+                    for d in ds:
+                        send(mine, mine, l2_s.at[k], l2_r.at[pair], zdev(lax.rem(z + d, 8)))
 
     def relay_factor(i):
         @pl.when(n == (i + 2) % 4)
         def _():
-            for k in range(i):
+            own = range(1, 3) if i == 3 else range(i)
+            for k in own:
                 pair = i * (i - 1) // 2 + k
                 settle(l_buf.at[pair], l2_r.at[pair])
-                for d in (1, 7):
-                    origin = lax.rem(z + (6 if d == 1 else 2), 8) // 4
-                    held = l_buf.at[pair, :, origin]
-                    send(held, held, l3_s.at[k], l2_r.at[pair], zdev(lax.rem(z + d, 8)))
-
-                    @pl.when(c == d // 7)
-                    def _(d=d, held=held):
-                        send(held, held, l3_s.at[k], l2_r.at[pair], zdev(lax.rem(z + (2 if d == 1 else 6), 8)))
-
-    forward_factor(1)
-    forward_factor(2)
-    arrived_inverse(1)
-    forward_inverse(1, False)
+            for far in range(2):
+                for k in own:
+                    pair = i * (i - 1) // 2 + k
+                    for side in range(2):
+                        held = l_buf.at[pair, :, lax.rem(z + (2 if side else 6), 8) // 4]
+                        hops = 1 + far
+
+                        @pl.when(c == side if far else c < 2)
+                        def _(held=held, hops=hops, side=side, k=k, pair=pair):
+                            send(held, held, l3_s.at[k], l2_r.at[pair], zdev(lax.rem(z + (8 - hops if side else hops), 8)))
+
+    def send_first(parts):
+        for g in range(2):
+            piece = jnp.concatenate([p[:, g * 64:(g + 1) * 64] for p in parts], axis=1)
+            away_src[g] = piece
+            here = jnp.logical_and(n == 3, zh == g)
+
+            @pl.when(here)
+            def _(piece=piece):
+                away_buf[z] = piece
+
+            @pl.when(jnp.logical_not(here))
+            def _(g=g):
+                send(away_src.at[g], away_buf.at[z], away_sem.at[0], away_sem.at[1], dev(g, x, y, c, 3))
+
+    def multiply_first():
+        @pl.when(n == 3)
+        def _():
+            own_fac(0).wait()
+            settle(y_buf.at[0, pl.ds(0, 7)], l1_r.at[0])
+            settle(away_buf.at[pl.ds(0, 7)], away_sem.at[1])
+            hi, lo = split(away_buf[...].reshape(128, 128))
+            w_hi, w_lo = split(l_buf[3, :, zh].reshape(128, 128))
+            d = jnp.dot(jnp.concatenate([hi, lo], axis=0), jnp.concatenate([w_hi, w_lo], axis=1), preferred_element_type=F32)
+            back_src[...] = (d[0:128, 0:128] + d[128:256, 128:256]) + (d[0:128, 128:256] + d[128:256, 0:128])
+            back_buf[zh] = back_src[pl.ds(pl.multiple_of(z * 16, 16), 16), :]
+            for m in (4, 3, 5, 2, 6, 1, 7):
+                to = lax.rem(z + m, 8)
+                send(back_src.at[pl.ds(pl.multiple_of(to * 16, 16), 16), :], back_buf.at[zh], back_sem.at[0], back_sem.at[1],
+                     zdev(to))
+
+    def returned():
+        @pl.when(n == 3)
+        def _():
+            settle(back_buf.at[0], back_sem.at[1])
+
+        @pl.when(n != 3)
+        def _():
+            settle(back_buf, back_sem.at[1])
+        return back_buf[0] + back_buf[1]
+
+    def pass_on(point):
+        for what, *args in PLAN[point]:
+            {"f": forward_factor, "r": relay_factor, "m": multiply_first, "i": forward_inverse, "j": relay_inverse,
+             "a": arrived_inverse, "s": start_inverse, "d": direct_inverse}[what](*args)
+
+    pass_on("gather")
 
     def split(v):
         hi = v.astype(BF16)
@@ -196,11 +288,13 @@
     def prepare_factor(i, k):
         pair = i * (i - 1) // 2 + k
 
+        passes_on = -1 if i == 1 else (i + 2) % 4
+
         @pl.when(n == i)
         def _():
             settle(l_buf.at[pair, :, 0], l2_r.at[pair])
 
-        @pl.when(jnp.logical_and(n != i, n != (i + 2) % 4))
+        @pl.when(jnp.logical_and(n != i, n != passes_on))
         def _():
             settle(l_buf.at[pair], l2_r.at[pair])
         hi, lo = split(l_buf[pair].reshape(256, 128))
@@ -264,6 +358,7 @@
                 send(rows, o_buf.at[z], o_s.at[i], o_r.at[0], dev(g, x, y, c, i))
 
     prepare_inverse(0)
+    pass_on("gather end")
     settle(p1_buf.at[pl.ds(0, 7)], p1_sem.at[1])
     lane_window = lax.broadcasted_iota(jnp.int32, (16, 128), 1) // 16
 
@@ -279,56 +374,58 @@
 
     gathered(0)
     send_x(0, apply_inverse(0, g_all[0]))
-    relay_factor(1)
-    forward_factor(3)
-    relay_inverse(1)
+    pass_on("x0")
     for i in range(1, 4):
         gathered(i)
+    pass_on("x0 end")
     prepare_factor(1, 0)
     parts = solved_parts(0)
 
     for i in range(1, 4):
-        ahead = None
-        for k in range(i - 1):
+        ahead = returned() if i == 3 else None
+        for k in range(1 if i == 3 else 0, i - 1):
             term = apply_factor(i, k)
             ahead = term if ahead is None else ahead + term
         last = apply_factor(i, i - 1)
         send_y(i - 1, last if ahead is None else ahead + last)
         send_out(i - 1, parts)
         if i == 1:
-            relay_factor(2)
-        if i < 3:
-            forward_inverse(i + 1, False)
+            send_first(parts)
+        pass_on(f"y{i - 1}")
+        pass_on(f"y{i - 1} end")
         prepare_inverse(i)
         settle(y_buf.at[i - 1, pl.ds(0, 7)], y_sem.at[1, i - 1])
         sums = halves(y_buf, i - 1)
         partial = apply_inverse(i, g_all[i] - jnp.concatenate(sums, axis=1))
         if i < 3:
             send_x(i, partial)
-            relay_inverse(i + 1)
-            if i == 1:
-                relay_factor(3)
-            for k in range(i + 1):
+            pass_on(f"x{i}")
+            pass_on(f"x{i} end")
+            for k in range(1 if i == 2 else 0, i + 1):
                 prepare_factor(i + 1, k)
             parts = solved_parts(i)
 
-    o_src[3] = spread_cases(partial)
+    low = lax.rem(lax.broadcasted_iota(jnp.int32, (16, 128), 1) // 8, 2) == 0
+    spread[pl.ds(pl.multiple_of(z * 16, 16), 16), :] = jnp.where(low, partial, 0.0)
+    spread[pl.ds(pl.multiple_of((1 - zh) * 64 + n * 16, 16), 16), :] = jnp.where(low, 0.0, partial)
+    wide_rows = spread[...].T.reshape(8, 2, 8, 128)
+    f_src[...] = (wide_rows[:, 0] + wide_rows[:, 1]).reshape(64, 128)
     for g in range(2):
         for d in (2, 1, 3, 0):
             xt = lax.rem(x + d, 4)
-            at = pl.ds(pl.multiple_of((g * 4 + xt) * 16, 16), 16)
+            at = pl.ds(pl.multiple_of((g * 4 + xt) * 8, 8), 8)
             if d:
-                send(o_src.at[3, at, :], f_buf.at[z * 4 + x], o_s.at[3], o_r.at[1], dev(g, xt, y, c, 3))
+                send(f_src.at[at, :], f_buf.at[z * 4 + x], o_s.at[3], o_r.at[1], dev(g, xt, y, c, 3))
             else:
                 own_place = jnp.logical_and(n == 3, zh == g)
 
                 @pl.when(own_place)
                 def _():
-                    f_buf[z * 4 + x] = o_src[3, at, :]
+                    f_buf[z * 4 + x] = f_src[at, :]
 
                 @pl.when(jnp.logical_not(own_place))
                 def _():
-                    send(o_src.at[3, at, :], f_buf.at[z * 4 + x], o_s.at[3], o_r.at[1], dev(g, xt, y, c, 3))
+                    send(f_src.at[at, :], f_buf.at[z * 4 + x], o_s.at[3], o_r.at[1], dev(g, xt, y, c, 3))
 
     def drain_weights():
         settle(inv_buf.at[0, :, pl.ds(0, 3)], i1_sem.at[0, 0])
@@ -342,11 +439,32 @@
             @pl.when(k < n)
             def _(k=k):
                 settle(y_buf.at[0, pl.ds(0, 7)], l1_s.at[k])
-                settle(l_buf.at[pl.ds(0, 2)], l2_s.at[k])
-
-            @pl.when(k < lax.rem(n + 2, 4))
-            def _(k=k):
-                settle(inv_buf.at[:, :, pl.ds(0, 3)], l3_s.at[k])
+
+        @pl.when(n == 1)
+        def _():
+            settle(inv_buf.at[:, :, pl.ds(0, 7)], l2_s.at[0])
+
+        for i in range(2, 4):
+            own = range(1, 3) if i == 3 else range(i)
+
+            @pl.when(n == i)
+            def _(own=own):
+                for k in own:
+                    settle(l_buf.at[pl.ds(0, 2)], l2_s.at[k])
+
+            @pl.when(n == (i + 2) % 4)
+            def _(own=own):
+                for k in own:
+                    settle(inv_buf.at[:, :, pl.ds(0, 3)], l3_s.at[k])
+
+        @pl.when(n == 3)
+        def _():
+            settle(away_src.at[0], away_sem.at[0])
+            settle(away_buf.at[pl.ds(0, 7)], back_sem.at[0])
+
+        @pl.when(n != 3)
+        def _():
+            settle(away_src, away_sem.at[0])
 
     drain_weights()
     settle(p0_buf.at[pl.ds(0, 7)], p0_sem.at[0])
@@ -357,14 +475,15 @@
 
     for i in range(4):
         count = 2 if i < 3 else 8
+        sized = o_buf if i < 3 else f_buf
 
         @pl.when(n == i)
-        def _(i=i, count=count):
-            settle(f_buf.at[pl.ds(0, count - 1)], o_s.at[i])
+        def _(i=i, count=count, sized=sized):
+            settle(sized.at[pl.ds(0, count - 1)], o_s.at[i])
 
         @pl.when(n != i)
-        def _(i=i, count=count):
-            settle(f_buf.at[pl.ds(0, count)], o_s.at[i])
+        def _(i=i, count=count, sized=sized):
+            settle(sized.at[pl.ds(0, count)], o_s.at[i])
 
     @pl.when(n < 3)
     def _():
@@ -377,10 +496,15 @@
     @pl.when(n == 3)
     def _():
         settle(f_buf.at[pl.ds(0, 31)], o_r.at[1])
-        total = f_buf[0]
-        for k in range(1, 32):
-            total = total + f_buf[k]
-        out_ref[...] = total
+        groups = []
+        for first in (0, 16):
+            total = f_buf[first]
+            for k in range(1, 16):
+                total = total + f_buf[first + k]
+            groups.append(total)
+        left = lax.broadcasted_iota(jnp.int32, (8, 128), 1) < 64
+        out_ref[0:8, :] = jnp.where(left, groups[0], groups[1])
+        out_ref[8:16, :] = pltpu.roll(jnp.where(left, groups[1], groups[0]), 64, 1)
 
 
 def body(factor_rows, load_vectors, child_updates, block_inverses):
@@ -400,10 +524,12 @@
             pltpu.VMEM((4, 2, 8, 16, 128), F32), pltpu.VMEM((4, 256, 256), BF16),
             pltpu.VMEM((6, 2, 2, 4, 16, 128), F32), pltpu.VMEM((6, 256, 256), BF16),
             pltpu.VMEM((3, 32, 256), BF16),
-            pltpu.VMEM((128, 128), F32), pltpu.VMEM((4, 128, 128), F32),
-            pltpu.VMEM((8, 16, 128), F32), pltpu.VMEM((32, 16, 128), F32),
+            pltpu.VMEM((128, 128), F32), pltpu.VMEM((3, 128, 128), F32),
+            pltpu.VMEM((8, 16, 128), F32), pltpu.VMEM((32, 8, 128), F32), pltpu.VMEM((64, 128), F32),
+            pltpu.VMEM((2, 16, 128), F32), pltpu.VMEM((8, 16, 128), F32),
+            pltpu.VMEM((128, 128), F32), pltpu.VMEM((2, 16, 128), F32),
             dma((7,)), dma((2,)), dma((2,)), dma((2, 3)), dma((2, 3)), dma((2, 2)),
-            dma, dma((4,)), dma((3,)), dma((3,)), dma((3,)), dma((6,)), dma((3,)), dma((4,)), dma((2,)),
+            dma, dma((4,)), dma((3,)), dma((3,)), dma((3,)), dma((6,)), dma((3,)), dma((2,)), dma((2,)), dma((4,)), dma((2,)),
         ],
         compiler_params=pltpu.CompilerParams(collective_id=0, has_side_effects=True, vmem_limit_bytes=60 << 20),
         name="substitution",

time: 56.1 us -> 51.6 us (0.920)
  Pallas kernels: 54.6 us -> 50.1 us
    pallas_call x1, Pallas kernels: 54.6 us -> 50.1 us  [body(): pl.pallas_call(kernel, out_shape=jax.ShapeDtypeStruct((16, 128), F32), in...]
where the time goes in v3:
time: 51.6 us; the launch traced here: 51.4 us
  Pallas kernels  50.1 us (97%)
  local copies, waits for them, and re-layouts  1.3 us (3%)
    pallas_call x1, Pallas kernels, body(): pl.pallas_call(kernel, out_shape=jax.ShapeDtypeStruct((16, 128), F32), in...  50.1 us
    unnamed x1, local copies, waits for them, and re-layouts  1.3 us

profile of v3, /device:TPU:96, one launch (start us, length us, event | category | flops | bytes accessed | tf_op | source)
XLA Modules:
  0.0 51.4 jit_solution(12151787134798735535)
XLA Ops:
  0.0 50.1 %substitution.1 = f32[16,128]{1,0:T(8,128)} custom-call(f32[4,16,1024]{2,1,0:T(8,128)} %inv_ref.1, f32[4,16,1024]{2,1,0:T(8,128)} %bitcast.4, f32[16,128]{1,0:T(8,128)} %bitcast.7, f32[4,16,128]{2,1,0:T(8,128)} %bitcast.6), custom_call_target="tpu_custom_call" | custom-call | tf_op jit(solution)/shard_map/substitution/pallas_call | solution.py:512
  50.1 1.3 %copy.6 = f32[1,1,16,128]{3,2,1,0:T(8,128)} copy(f32[1,1,16,128]{3,2,1,0:T(8,128)} %bitcast.5) | data formatting | bytes 16384

commit v4 on v3

--- a/solution.py
+++ b/solution.py
@@ -11,19 +11,20 @@
 PLAN = {
     "gather": [("f", 1), ("f", 2), ("s", 1), ("d", 1, False)],
     "gather end": [],
-    "x0": [("f", 3)],
-    "x0 end": [("a", 1), ("j", 1)],
+    "x0": [],
+    "x0 end": [("a", 1), ("j", 1), ("f", 3)],
     "y0": [("r", 2), ("i", 2, False)],
     "y0 end": [],
     "x1": [],
-    "x1 end": [("j", 2), ("m",), ("r", 3)],
-    "y1": [("i", 3, False)],
+    "x1 end": [("j", 2)],
+    "y1": [("m",), ("r", 3), ("i", 3, False)],
     "y1 end": [],
     "x2": [],
     "x2 end": [("j", 3)],
     "y2": [],
     "y2 end": [],
 }
+WHOLE = (0,)
 
 
 def kernel(inv_ref, fac_ref, load_ref, child_ref, out_ref,
@@ -274,7 +275,7 @@
         return hi, (v - hi.astype(F32)).astype(BF16)
 
     def prepare_inverse(i):
-        if i == 0:
+        if i in WHOLE:
             settle(inv_buf.at[i, :, pl.ds(0, 4)], i2_r.at[i])
         else:
             @pl.when(jnp.logical_and(n != 0, n != 3))
@@ -388,9 +389,9 @@
             ahead = term if ahead is None else ahead + term
         last = apply_factor(i, i - 1)
         send_y(i - 1, last if ahead is None else ahead + last)
-        send_out(i - 1, parts)
         if i == 1:
             send_first(parts)
+        send_out(i - 1, parts)
         pass_on(f"y{i - 1}")
         pass_on(f"y{i - 1} end")
         prepare_inverse(i)

time: 51.6 us -> 49.2 us (0.953)
  Pallas kernels: 50.1 us -> 47.7 us
    pallas_call x1, Pallas kernels: 50.1 us -> 47.7 us  [body(): pl.pallas_call(kernel, out_shape=jax.ShapeDtypeStruct((16, 128), F32), in...]
where the time goes in v4:
time: 49.2 us; the launch traced here: 49 us
  Pallas kernels  47.7 us (97%)
  local copies, waits for them, and re-layouts  1.3 us (3%)
    pallas_call x1, Pallas kernels, body(): pl.pallas_call(kernel, out_shape=jax.ShapeDtypeStruct((16, 128), F32), in...  47.7 us
    unnamed x1, local copies, waits for them, and re-layouts  1.3 us

profile of v4, /device:TPU:96, one launch (start us, length us, event | category | flops | bytes accessed | tf_op | source)
XLA Modules:
  0.0 49.0 jit_solution(6158947156013689231)
XLA Ops:
  0.0 47.7 %substitution.1 = f32[16,128]{1,0:T(8,128)} custom-call(f32[4,16,1024]{2,1,0:T(8,128)} %inv_ref.1, f32[4,16,1024]{2,1,0:T(8,128)} %bitcast.4, f32[16,128]{1,0:T(8,128)} %bitcast.7, f32[4,16,128]{2,1,0:T(8,128)} %bitcast.6), custom_call_target="tpu_custom_call" | custom-call | tf_op jit(solution)/shard_map/substitution/pallas_call | solution.py:513
  47.7 1.3 %copy.6 = f32[1,1,16,128]{3,2,1,0:T(8,128)} copy(f32[1,1,16,128]{3,2,1,0:T(8,128)} %bitcast.5) | data formatting | bytes 16384

commit v5 on v4

--- a/solution.py
+++ b/solution.py
@@ -380,15 +380,16 @@
         gathered(i)
     pass_on("x0 end")
     prepare_factor(1, 0)
+    ahead = None
     parts = solved_parts(0)
 
     for i in range(1, 4):
-        ahead = returned() if i == 3 else None
-        for k in range(1 if i == 3 else 0, i - 1):
-            term = apply_factor(i, k)
-            ahead = term if ahead is None else ahead + term
-        last = apply_factor(i, i - 1)
-        send_y(i - 1, last if ahead is None else ahead + last)
+        total = apply_factor(i, i - 1)
+        if i > 1:
+            total = ahead + total
+        if i == 3:
+            total = returned() + total
+        send_y(i - 1, total)
         if i == 1:
             send_first(parts)
         send_out(i - 1, parts)
@@ -404,6 +405,7 @@
             pass_on(f"x{i} end")
             for k in range(1 if i == 2 else 0, i + 1):
                 prepare_factor(i + 1, k)
+            ahead = apply_factor(i + 1, i - 1)
             parts = solved_parts(i)
 
     low = lax.rem(lax.broadcasted_iota(jnp.int32, (16, 128), 1) // 8, 2) == 0
@@ -411,22 +413,22 @@
     spread[pl.ds(pl.multiple_of((1 - zh) * 64 + n * 16, 16), 16), :] = jnp.where(low, 0.0, partial)
     wide_rows = spread[...].T.reshape(8, 2, 8, 128)
     f_src[...] = (wide_rows[:, 0] + wide_rows[:, 1]).reshape(64, 128)
-    for g in range(2):
-        for d in (2, 1, 3, 0):
-            xt = lax.rem(x + d, 4)
-            at = pl.ds(pl.multiple_of((g * 4 + xt) * 8, 8), 8)
-            if d:
+    far = jnp.where(n < 2, zh, 1 - zh)
+    for d, g in [(d, far) for d in (2, 1, 3, 0)] + [(d, 1 - far) for d in (2, 1, 3, 0)]:
+        xt = lax.rem(x + d, 4)
+        at = pl.ds(pl.multiple_of((g * 4 + xt) * 8, 8), 8)
+        if d:
+            send(f_src.at[at, :], f_buf.at[z * 4 + x], o_s.at[3], o_r.at[1], dev(g, xt, y, c, 3))
+        else:
+            own_place = jnp.logical_and(n == 3, zh == g)
+
+            @pl.when(own_place)
+            def _(at=at):
+                f_buf[z * 4 + x] = f_src[at, :]
+
+            @pl.when(jnp.logical_not(own_place))
+            def _(at=at, xt=xt, g=g):
                 send(f_src.at[at, :], f_buf.at[z * 4 + x], o_s.at[3], o_r.at[1], dev(g, xt, y, c, 3))
-            else:
-                own_place = jnp.logical_and(n == 3, zh == g)
-
-                @pl.when(own_place)
-                def _():
-                    f_buf[z * 4 + x] = f_src[at, :]
-
-                @pl.when(jnp.logical_not(own_place))
-                def _():
-                    send(f_src.at[at, :], f_buf.at[z * 4 + x], o_s.at[3], o_r.at[1], dev(g, xt, y, c, 3))
 
     def drain_weights():
         settle(inv_buf.at[0, :, pl.ds(0, 3)], i1_sem.at[0, 0])
@@ -512,7 +514,7 @@
     dma = pltpu.SemaphoreType.DMA
     out = pl.pallas_call(
         kernel,
-        out_shape=jax.ShapeDtypeStruct((16, 128), F32),
+        out_shape=pltpu.VMEM((16, 128), F32),
         in_specs=[pl.BlockSpec(memory_space=pltpu.HBM)] * 4,
         out_specs=pl.BlockSpec(memory_space=pltpu.VMEM),
         scratch_shapes=[

time: 49.2 us -> 47.9 us (0.974)
  local copies, waits for them, and re-layouts: 1.3 us -> 0.6 us
  Pallas kernels: 47.7 us -> 47.2 us
    unnamed x1, local copies, waits for them, and re-layouts: 1.3 us -> 0.6 us
    pallas_call x1, Pallas kernels: 47.7 us -> 47.2 us  [body(): pl.pallas_call(kernel, out_shape=pltpu.VMEM((16, 128), F32), in_specs=[pl...]
where the time goes in v5:
time: 47.9 us; the launch traced here: 47.8 us
  Pallas kernels  47.2 us (99%)
  local copies, waits for them, and re-layouts  0.6 us (1%)
    pallas_call x1, Pallas kernels, body(): pl.pallas_call(kernel, out_shape=pltpu.VMEM((16, 128), F32), in_specs=[pl...  47.2 us

profile of v5, /device:TPU:96, one launch (start us, length us, event | category | flops | bytes accessed | tf_op | source)
XLA Modules:
  0.0 47.8 jit_solution(8492755077295374112)
XLA Ops:
  0.0 47.2 %substitution.1 = f32[16,128]{1,0:T(8,128)S(1)} custom-call(f32[4,16,1024]{2,1,0:T(8,128)} %inv_ref.1, f32[4,16,1024]{2,1,0:T(8,128)} %bitcast.5, f32[16,128]{1,0:T(8,128)} %bitcast.7, f32[4,16,128]{2,1,0:T(8,128)} %bitcast.6), custom_call_target="tpu_custom_call" | custom-call | tf_op jit(solution)/shard_map/substitution/pallas_call | solution.py:515
  47.2 0.6 %copy.6 = f32[1,1,16,128]{3,2,1,0:T(8,128)} copy(f32[1,1,16,128]{3,2,1,0:T(8,128)S(1)} %bitcast.4) | data formatting | bytes 16384

commit v6 on v5

--- a/solution.py
+++ b/solution.py
@@ -9,11 +9,12 @@
 F32, BF16 = jnp.float32, jnp.bfloat16
 
 PLAN = {
-    "gather": [("f", 1), ("f", 2), ("s", 1), ("d", 1, False)],
+    "enter": [("f", 1)],
+    "gather": [("f", 2), ("s", 1), ("d", 1, False)],
     "gather end": [],
     "x0": [],
-    "x0 end": [("a", 1), ("j", 1), ("f", 3)],
-    "y0": [("r", 2), ("i", 2, False)],
+    "x0 end": [("a", 1), ("j", 1), ("f", 3), ("r", 2)],
+    "y0": [("i", 2, False)],
     "y0 end": [],
     "x1": [],
     "x1 end": [("j", 2)],
@@ -152,8 +153,12 @@
                                  dev(1 - zh, xt, y, c, lane))
 
     direct_inverse(0, True)
-    start_inverse(0)
-    start_factor()
+    for part in range(2):
+        @pl.when(n == 1 if part == 0 else n > 1)
+        def _():
+            start_factor()
+        if part == 0:
+            start_inverse(0)
 
     def arrived_inverse(part):
         settle(inv_buf.at[pl.ds(part, 1 + 2 * part), :, pl.ds(0, 3)], i1_sem.at[1, part])
@@ -181,15 +186,6 @@
     for cp in own_inv:
         cp.wait()
     arrived_inverse(0)
-
-    settle(p0_buf.at[pl.ds(0, 7)], p0_sem.at[1])
-    own = p0_buf[0]
-    for k in range(1, 8):
-        own = own + p0_buf[k]
-    p1_src[...] = own
-    p1_buf[yc] = own
-    for d, e in ring:
-        send(p1_src, p1_buf.at[yc], p1_sem.at[0], p1_sem.at[1], dev(zh, x, lax.rem(y + d, 4), lax.rem(c + e, 2), n))
 
     def forward_factor(i):
         @pl.when(n == i)
@@ -267,6 +263,17 @@
         for what, *args in PLAN[point]:
             {"f": forward_factor, "r": relay_factor, "m": multiply_first, "i": forward_inverse, "j": relay_inverse,
              "a": arrived_inverse, "s": start_inverse, "d": direct_inverse}[what](*args)
+
+    pass_on("enter")
+
+    settle(p0_buf.at[pl.ds(0, 7)], p0_sem.at[1])
+    own = p0_buf[0]
+    for k in range(1, 8):
+        own = own + p0_buf[k]
+    p1_src[...] = own
+    p1_buf[yc] = own
+    for d, e in ring:
+        send(p1_src, p1_buf.at[yc], p1_sem.at[0], p1_sem.at[1], dev(zh, x, lax.rem(y + d, 4), lax.rem(c + e, 2), n))
 
     pass_on("gather")
 

time: 47.9 us -> 46.9 us (0.979)
  Pallas kernels: 47.2 us -> 46.2 us
    pallas_call x1, Pallas kernels: 47.2 us -> 46.2 us  [body(): pl.pallas_call(kernel, out_shape=pltpu.VMEM((16, 128), F32), in_specs=[pl...]
where the time goes in v6:
time: 46.9 us; the launch traced here: 46.8 us
  Pallas kernels  46.2 us (99%)
  local copies, waits for them, and re-layouts  0.6 us (1%)
    pallas_call x1, Pallas kernels, body(): pl.pallas_call(kernel, out_shape=pltpu.VMEM((16, 128), F32), in_specs=[pl...  46.2 us

profile of v6, /device:TPU:96, one launch (start us, length us, event | category | flops | bytes accessed | tf_op | source)
XLA Modules:
  0.0 46.8 jit_solution(4697737965886210440)
XLA Ops:
  0.0 46.2 %substitution.1 = f32[16,128]{1,0:T(8,128)S(1)} custom-call(f32[4,16,1024]{2,1,0:T(8,128)} %inv_ref.1, f32[4,16,1024]{2,1,0:T(8,128)} %bitcast.5, f32[16,128]{1,0:T(8,128)} %bitcast.7, f32[4,16,128]{2,1,0:T(8,128)} %bitcast.6), custom_call_target="tpu_custom_call" | custom-call | tf_op jit(solution)/shard_map/substitution/pallas_call | solution.py:522
  46.2 0.6 %copy.6 = f32[1,1,16,128]{3,2,1,0:T(8,128)} copy(f32[1,1,16,128]{3,2,1,0:T(8,128)S(1)} %bitcast.4) | data formatting | bytes 16384

commit v7 on v6

--- a/solution.py
+++ b/solution.py
@@ -10,10 +10,10 @@
 
 PLAN = {
     "enter": [("f", 1)],
-    "gather": [("f", 2), ("s", 1), ("d", 1, False)],
+    "gather": [("f", 2), ("s", 1), ("d", 1, True)],
     "gather end": [],
     "x0": [],
-    "x0 end": [("a", 1), ("j", 1), ("f", 3), ("r", 2)],
+    "x0 end": [("a", 1), ("f", 3), ("r", 2)],
     "y0": [("i", 2, False)],
     "y0 end": [],
     "x1": [],
@@ -25,7 +25,7 @@
     "y2": [],
     "y2 end": [],
 }
-WHOLE = (0,)
+WHOLE = (0, 1)
 
 
 def kernel(inv_ref, fac_ref, load_ref, child_ref, out_ref,

time: 46.9 us -> 46.9 us (level)
  no operation moved by 1% of the time
where the time goes in v7:
time: 46.9 us; the launch traced here: 46.8 us
  Pallas kernels  46.2 us (99%)
  local copies, waits for them, and re-layouts  0.6 us (1%)
    pallas_call x1, Pallas kernels, body(): pl.pallas_call(kernel, out_shape=pltpu.VMEM((16, 128), F32), in_specs=[pl...  46.2 us

profile of v7, /device:TPU:96, one launch (start us, length us, event | category | flops | bytes accessed | tf_op | source)
XLA Modules:
  0.0 46.8 jit_solution(3234666314210599388)
XLA Ops:
  0.0 46.2 %substitution.1 = f32[16,128]{1,0:T(8,128)S(1)} custom-call(f32[4,16,1024]{2,1,0:T(8,128)} %inv_ref.1, f32[4,16,1024]{2,1,0:T(8,128)} %bitcast.5, f32[16,128]{1,0:T(8,128)} %bitcast.7, f32[4,16,128]{2,1,0:T(8,128)} %bitcast.6), custom_call_target="tpu_custom_call" | custom-call | tf_op jit(solution)/shard_map/substitution/pallas_call | solution.py:522
  46.2 0.6 %copy.6 = f32[1,1,16,128]{3,2,1,0:T(8,128)} copy(f32[1,1,16,128]{3,2,1,0:T(8,128)S(1)} %bitcast.4) | data formatting | bytes 16384

commit v8 on v7

--- a/solution.py
+++ b/solution.py
@@ -18,14 +18,14 @@
     "y0 end": [],
     "x1": [],
     "x1 end": [("j", 2)],
-    "y1": [("m",), ("r", 3), ("i", 3, False)],
+    "y1": [("m",), ("r", 3), ("i", 3, True)],
     "y1 end": [],
     "x2": [],
-    "x2 end": [("j", 3)],
+    "x2 end": [],
     "y2": [],
     "y2 end": [],
 }
-WHOLE = (0, 1)
+WHOLE = (0, 1, 3)
 
 
 def kernel(inv_ref, fac_ref, load_ref, child_ref, out_ref,

time: 46.9 us -> 46.9 us (level)
  no operation moved by 1% of the time
where the time goes in v8:
time: 46.9 us; the launch traced here: 46.8 us
  Pallas kernels  46.2 us (99%)
  local copies, waits for them, and re-layouts  0.6 us (1%)
    pallas_call x1, Pallas kernels, body(): pl.pallas_call(kernel, out_shape=pltpu.VMEM((16, 128), F32), in_specs=[pl...  46.2 us

profile of v8, /device:TPU:96, one launch (start us, length us, event | category | flops | bytes accessed | tf_op | source)
XLA Modules:
  0.0 46.8 jit_solution(6201602795042978947)
XLA Ops:
  0.0 46.2 %substitution.1 = f32[16,128]{1,0:T(8,128)S(1)} custom-call(f32[4,16,1024]{2,1,0:T(8,128)} %inv_ref.1, f32[4,16,1024]{2,1,0:T(8,128)} %bitcast.5, f32[16,128]{1,0:T(8,128)} %bitcast.7, f32[4,16,128]{2,1,0:T(8,128)} %bitcast.6), custom_call_target="tpu_custom_call" | custom-call | tf_op jit(solution)/shard_map/substitution/pallas_call | solution.py:522
  46.2 0.6 %copy.6 = f32[1,1,16,128]{3,2,1,0:T(8,128)} copy(f32[1,1,16,128]{3,2,1,0:T(8,128)S(1)} %bitcast.4) | data formatting | bytes 16384

commit v9 on v7

--- a/solution.py
+++ b/solution.py
@@ -59,18 +59,25 @@
     ring = [(2, 0), (2, 1), (1, 0), (1, 1), (3, 0), (3, 1), (0, 1)]
 
     barrier = pltpu.get_barrier_semaphore()
-    for d in (4, 3, 5, 2, 6, 1, 7):
-        pl.semaphore_signal(barrier, inc=1, device_id=zdev(lax.rem(z + d, 8)), device_id_type=MESH)
+    near = jnp.where(n < 2, 3, 0)
+
+    def greet(to):
+        pl.semaphore_signal(barrier, inc=1, device_id=to, device_id_type=MESH)
+
+    greet(zdev(lax.rem(z + 4, 8)))
+    greet(dev(1 - zh, lax.rem(x + 2, 4), y, c, near))
+    for d in (3, 5):
+        greet(zdev(lax.rem(z + d, 8)))
+    for d in (1, 3):
+        greet(dev(1 - zh, lax.rem(x + d, 4), y, c, near))
+    for d in (2, 6):
+        greet(zdev(lax.rem(z + d, 8)))
     for d, e in ring:
-        pl.semaphore_signal(barrier, inc=1, device_id=dev(zh, x, lax.rem(y + d, 4), lax.rem(c + e, 2), n),
-                            device_id_type=MESH)
+        greet(dev(zh, x, lax.rem(y + d, 4), lax.rem(c + e, 2), n))
     for d, e in ring[:-1]:
-        pl.semaphore_signal(barrier, inc=1, device_id=dev(zh, lax.rem(x + d, 4), y, lax.rem(c + e, 2), n),
-                            device_id_type=MESH)
-
-    near = jnp.where(n < 2, 3, 0)
-    for d in (2, 1, 3):
-        pl.semaphore_signal(barrier, inc=1, device_id=dev(1 - zh, lax.rem(x + d, 4), y, c, near), device_id_type=MESH)
+        greet(dev(zh, lax.rem(x + d, 4), y, lax.rem(c + e, 2), n))
+    for d in (1, 7):
+        greet(zdev(lax.rem(z + d, 8)))
     at_end = jnp.logical_or(n == 0, n == 3)
 
     kid_in = pltpu.make_async_copy(child_ref, kid_v, loc_sem.at[0])
@@ -415,27 +422,28 @@
             ahead = apply_factor(i + 1, i - 1)
             parts = solved_parts(i)
 
-    low = lax.rem(lax.broadcasted_iota(jnp.int32, (16, 128), 1) // 8, 2) == 0
-    spread[pl.ds(pl.multiple_of(z * 16, 16), 16), :] = jnp.where(low, partial, 0.0)
-    spread[pl.ds(pl.multiple_of((1 - zh) * 64 + n * 16, 16), 16), :] = jnp.where(low, 0.0, partial)
-    wide_rows = spread[...].T.reshape(8, 2, 8, 128)
-    f_src[...] = (wide_rows[:, 0] + wide_rows[:, 1]).reshape(64, 128)
+    quad = lax.rem(lax.broadcasted_iota(jnp.int32, (16, 128), 1) // 4, 4)
+    for j in range(4):
+        spread[pl.ds(pl.multiple_of(lax.rem(z + 2 * j, 8) * 16, 16), 16), :] = jnp.where(quad == j, partial, 0.0)
+    eights = spread[...].T.reshape(8, 2, 8, 128)
+    eights = eights[:, 0] + eights[:, 1]
+    f_src[...] = eights[:, 0:4] + eights[:, 4:8]
     far = jnp.where(n < 2, zh, 1 - zh)
     for d, g in [(d, far) for d in (2, 1, 3, 0)] + [(d, 1 - far) for d in (2, 1, 3, 0)]:
         xt = lax.rem(x + d, 4)
-        at = pl.ds(pl.multiple_of((g * 4 + xt) * 8, 8), 8)
+        at = g * 4 + xt
         if d:
-            send(f_src.at[at, :], f_buf.at[z * 4 + x], o_s.at[3], o_r.at[1], dev(g, xt, y, c, 3))
+            send(f_src.at[at], f_buf.at[z * 4 + x], o_s.at[3], o_r.at[1], dev(g, xt, y, c, 3))
         else:
             own_place = jnp.logical_and(n == 3, zh == g)
 
             @pl.when(own_place)
             def _(at=at):
-                f_buf[z * 4 + x] = f_src[at, :]
+                f_buf[z * 4 + x] = f_src[at]
 
             @pl.when(jnp.logical_not(own_place))
             def _(at=at, xt=xt, g=g):
-                send(f_src.at[at, :], f_buf.at[z * 4 + x], o_s.at[3], o_r.at[1], dev(g, xt, y, c, 3))
+                send(f_src.at[at], f_buf.at[z * 4 + x], o_s.at[3], o_r.at[1], dev(g, xt, y, c, 3))
 
     def drain_weights():
         settle(inv_buf.at[0, :, pl.ds(0, 3)], i1_sem.at[0, 0])
@@ -507,14 +515,17 @@
     def _():
         settle(f_buf.at[pl.ds(0, 31)], o_r.at[1])
         groups = []
-        for first in (0, 16):
-            total = f_buf[first]
-            for k in range(1, 16):
-                total = total + f_buf[first + k]
+        for q in range(4):
+            total = f_buf[8 * q]
+            for k in range(1, 8):
+                total = total + f_buf[8 * q + k]
             groups.append(total)
-        left = lax.broadcasted_iota(jnp.int32, (8, 128), 1) < 64
-        out_ref[0:8, :] = jnp.where(left, groups[0], groups[1])
-        out_ref[8:16, :] = pltpu.roll(jnp.where(left, groups[1], groups[0]), 64, 1)
+        pair = lax.broadcasted_iota(jnp.int32, (4, 128), 1) // 32
+        for j in range(4):
+            rows = groups[0]
+            for q in range(1, 4):
+                rows = jnp.where(pair == (q + j) % 4, groups[q], rows)
+            out_ref[4 * j:4 * j + 4, :] = pltpu.roll(rows, (128 - 32 * j) % 128, 1) if j else rows
 
 
 def body(factor_rows, load_vectors, child_updates, block_inverses):
@@ -535,7 +546,7 @@
             pltpu.VMEM((6, 2, 2, 4, 16, 128), F32), pltpu.VMEM((6, 256, 256), BF16),
             pltpu.VMEM((3, 32, 256), BF16),
             pltpu.VMEM((128, 128), F32), pltpu.VMEM((3, 128, 128), F32),
-            pltpu.VMEM((8, 16, 128), F32), pltpu.VMEM((32, 8, 128), F32), pltpu.VMEM((64, 128), F32),
+            pltpu.VMEM((8, 16, 128), F32), pltpu.VMEM((32, 4, 128), F32), pltpu.VMEM((8, 4, 128), F32),
             pltpu.VMEM((2, 16, 128), F32), pltpu.VMEM((8, 16, 128), F32),
             pltpu.VMEM((128, 128), F32), pltpu.VMEM((2, 16, 128), F32),
             dma((7,)), dma((2,)), dma((2,)), dma((2, 3)), dma((2, 3)), dma((2, 2)),

time: 46.9 us -> 46.9 us (level)
  no operation moved by 1% of the time
where the time goes in v9:
time: 46.9 us; the launch traced here: 46.8 us
  Pallas kernels  46.2 us (99%)
  local copies, waits for them, and re-layouts  0.6 us (1%)
    pallas_call x1, Pallas kernels, body(): pl.pallas_call(kernel, out_shape=pltpu.VMEM((16, 128), F32), in_specs=[pl...  46.2 us

profile of v9, /device:TPU:96, one launch (start us, length us, event | category | flops | bytes accessed | tf_op | source)
XLA Modules:
  0.0 46.8 jit_solution(12855319159800768406)
XLA Ops:
  0.0 46.2 %substitution.1 = f32[16,128]{1,0:T(8,128)S(1)} custom-call(f32[4,16,1024]{2,1,0:T(8,128)} %inv_ref.1, f32[4,16,1024]{2,1,0:T(8,128)} %bitcast.5, f32[16,128]{1,0:T(8,128)} %bitcast.7, f32[4,16,128]{2,1,0:T(8,128)} %bitcast.6), custom_call_target="tpu_custom_call" | custom-call | tf_op jit(solution)/shard_map/substitution/pallas_call | solution.py:533
  46.2 0.6 %copy.6 = f32[1,1,16,128]{3,2,1,0:T(8,128)} copy(f32[1,1,16,128]{3,2,1,0:T(8,128)S(1)} %bitcast.4) | data formatting | bytes 16384

commit v10 on v7

--- a/solution.py
+++ b/solution.py
@@ -9,8 +9,8 @@
 F32, BF16 = jnp.float32, jnp.bfloat16
 
 PLAN = {
-    "enter": [("f", 1)],
-    "gather": [("f", 2), ("s", 1), ("d", 1, True)],
+    "enter": [("f", 1), ("f", 2)],
+    "gather": [("s", 1), ("d", 1, True)],
     "gather end": [],
     "x0": [],
     "x0 end": [("a", 1), ("f", 3), ("r", 2)],

time: 46.9 us -> 46.9 us (level)
  no operation moved by 1% of the time
where the time goes in v10:
time: 46.9 us; the launch traced here: 46.8 us
  Pallas kernels  46.2 us (99%)
  local copies, waits for them, and re-layouts  0.6 us (1%)
    pallas_call x1, Pallas kernels, body(): pl.pallas_call(kernel, out_shape=pltpu.VMEM((16, 128), F32), in_specs=[pl...  46.2 us

profile of v10, /device:TPU:96, one launch (start us, length us, event | category | flops | bytes accessed | tf_op | source)
XLA Modules:
  0.0 46.8 jit_solution(17049505813344397176)
XLA Ops:
  0.0 46.2 %substitution.1 = f32[16,128]{1,0:T(8,128)S(1)} custom-call(f32[4,16,1024]{2,1,0:T(8,128)} %inv_ref.1, f32[4,16,1024]{2,1,0:T(8,128)} %bitcast.5, f32[16,128]{1,0:T(8,128)} %bitcast.7, f32[4,16,128]{2,1,0:T(8,128)} %bitcast.6), custom_call_target="tpu_custom_call" | custom-call | tf_op jit(solution)/shard_map/substitution/pallas_call | solution.py:522
  46.2 0.6 %copy.6 = f32[1,1,16,128]{3,2,1,0:T(8,128)} copy(f32[1,1,16,128]{3,2,1,0:T(8,128)S(1)} %bitcast.4) | data formatting | bytes 16384
